TPU v7x, 256 devices: a whole 4x4x8 slice. The times are simulated.
256 devices in a mesh: dp: 8 (over y, core), ctx: 32 (over z, x).
Axes of the slice: x: 4, y: 4, z: 8, core: 2. Of those that a mesh axis runs over, the one named last changes fastest.
Arguments:
- q_in: bfloat16 [65536, 1024], P(('dp', 'ctx')), may hold values from -5 to 5
- k_in: bfloat16 [65536, 1024], P(('dp', 'ctx')), may hold values from -5 to 5
- v_in: bfloat16 [65536, 1024], P(('dp', 'ctx')), may hold values from -6 to 6
- cotangent: bfloat16 [65536, 2048], P(('dp', 'ctx')), may hold values from -1.796875 to 1.796875
- out_weight: bfloat16 [1024, 2048], replicated, may hold values from -0.1875 to 0.1875
- cluster_ids: int32 [8, 65536, 1], P(None, ('dp', 'ctx')), may hold values from 0 to 63; in each aligned block of 256 rows (0 to 255, 256 to 511, ..., all dimensions but the last counted through in order) at most 8 rows name the same one
Outputs:
- layer_out: bfloat16 [65536, 2048], P(('dp', 'ctx'))
- q_grad: bfloat16 [65536, 1024], P(('dp', 'ctx'))
- k_grad: bfloat16 [65536, 1024], P(('dp', 'ctx'))
- v_grad: bfloat16 [65536, 1024], P(('dp', 'ctx'))
- wo_grad: float32 [1024, 2048], P('ctx')
Inputs may be any that keep to these rules, and one draw needn't show every extreme that they name: `cluster_ids`: for each head, the 256 tokens of one device name any one cluster at most 8 times, a bound that some block reaches.
All inputs are finite; a program needn't handle non-finite values.
Results may differ from a plain program's by a relative error of at most 0.0085.
Values may be sent and summed in bfloat16 or wider, within the bound.
No kernel may reach another device: no remote copies, remote signals or barrier semaphores. Data moves between devices by JAX's collectives and lax.ppermute only.
A program may use at most 128 MiB of HBM per device.

v0:
```python
import math
import jax
import jax.numpy as jnp
from jax import lax
from jax.sharding import PartitionSpec as P

HEADS = 8
HEAD_DIM = 128
C_DEV = 2
SEQS = 1
NEG_FILL = -1e30


def attend_groups(query, keys_in, values_in, grad_out, position, filled, seq_length):
    score_scale = HEAD_DIM ** (-0.5)
    scores = (
        jnp.einsum("grd,gsd->grs", query, keys_in, preferred_element_type=jnp.float32) * score_scale
    )
    sequence = position // seq_length
    allowed = (
        filled[:, :, None]
        & filled[:, None, :]
        & (position[:, None, :] <= position[:, :, None])
        & (sequence[:, None, :] == sequence[:, :, None])
    )
    scores = jnp.where(allowed, scores, NEG_FILL)
    row_peak = jnp.max(scores, axis=-1, keepdims=True)
    exp_terms = jnp.exp(scores - row_peak)
    weights = exp_terms / jnp.sum(exp_terms, axis=-1, keepdims=True)
    weights_low = weights.astype(jnp.bfloat16)
    attended = jnp.einsum(
        "grs,gsd->grd", weights_low, values_in, preferred_element_type=jnp.float32
    ).astype(jnp.bfloat16)
    grad_prob = jnp.einsum("grd,gsd->grs", grad_out, values_in, preferred_element_type=jnp.float32)
    row_delta = jnp.sum(weights * grad_prob, axis=-1, keepdims=True)
    grad_score = (weights * (grad_prob - row_delta) * score_scale).astype(jnp.bfloat16)
    query_grad = jnp.einsum(
        "grs,gsd->grd", grad_score, keys_in, preferred_element_type=jnp.float32
    ).astype(jnp.bfloat16)
    key_grad = jnp.einsum(
        "grs,grd->gsd", grad_score, query, preferred_element_type=jnp.float32
    ).astype(jnp.bfloat16)
    value_grad = jnp.einsum(
        "grs,grd->gsd", weights_low, grad_out, preferred_element_type=jnp.float32
    ).astype(jnp.bfloat16)
    return (attended, query_grad, key_grad, value_grad)


def per_device(q_in, k_in, v_in, cotangent, out_weight, cluster_ids):
    ctx_size = lax.axis_size("ctx")
    dp_size = lax.axis_size("dp")
    tok_count = q_in.shape[0]
    clusters = C_DEV * ctx_size
    capacity = 2 * tok_count // clusters
    seq_length = tok_count * ctx_size // SEQS
    tok_iota = jnp.arange(tok_count, dtype=jnp.int32)
    lower_ones = (tok_iota[:, None] >= tok_iota[None, :]).astype(jnp.bfloat16)
    local_ids = cluster_ids[:, :, 0]
    cluster_hits = (local_ids[:, :, None] == jnp.arange(clusters, dtype=jnp.int32)).astype(
        jnp.bfloat16
    )
    running = jnp.einsum(
        "tu,huc->htc", lower_ones, cluster_hits, preferred_element_type=jnp.float32
    )
    rank_in_block = (jnp.sum(running * cluster_hits, axis=-1) - 1.0).astype(jnp.int32)
    slot_index = local_ids * capacity + rank_in_block
    dispatch = (slot_index[:, :, None] == jnp.arange(clusters * capacity, dtype=jnp.int32)).astype(
        jnp.bfloat16
    )
    grad_heads = lax.dot_general(
        cotangent, out_weight, (((1,), (1,)), ((), ())), preferred_element_type=jnp.float32
    ).astype(jnp.bfloat16)

    def to_slots(token_rows):
        per_head = token_rows.reshape(tok_count, HEADS, HEAD_DIM)
        slotted = jnp.einsum("hts,thd->hsd", dispatch, per_head, preferred_element_type=jnp.float32)
        return slotted.astype(jnp.bfloat16).reshape(HEADS, ctx_size, C_DEV, capacity, HEAD_DIM)

    query_slots = to_slots(q_in)
    key_slots = to_slots(k_in)
    value_slots = to_slots(v_in)
    grad_slots = to_slots(grad_heads)
    pieces = []
    for head_index in range(HEADS):
        pieces.append(
            (
                lax.all_to_all(
                    query_slots[head_index], "ctx", split_axis=0, concat_axis=2, tiled=True
                ),
                lax.all_to_all(
                    key_slots[head_index], "ctx", split_axis=0, concat_axis=2, tiled=True
                ),
                lax.all_to_all(
                    value_slots[head_index], "ctx", split_axis=0, concat_axis=2, tiled=True
                ),
                lax.all_to_all(
                    grad_slots[head_index], "ctx", split_axis=0, concat_axis=2, tiled=True
                ),
            )
        )
    arrived = tuple(
        (jnp.stack([piece_set[member_index] for piece_set in pieces]) for member_index in range(4))
    )
    group_count = C_DEV
    group_rows = ctx_size * capacity
    every_ids = lax.all_gather(cluster_ids, "ctx", axis=1, tiled=True)
    source_ids = every_ids[:, :, 0].reshape(HEADS, ctx_size, tok_count)
    owner_index = lax.axis_index("ctx")
    owned_hits = (
        source_ids[..., None] == owner_index * C_DEV + jnp.arange(C_DEV, dtype=jnp.int32)
    ).astype(jnp.bfloat16)
    owned_running = jnp.einsum(
        "tu,hsuc->hstc", lower_ones, owned_hits, preferred_element_type=jnp.float32
    )
    owned_rank = (owned_running - 1.0).astype(jnp.int32)
    slot_match = (owned_hits[..., None] > 0) & (
        owned_rank[..., None] == jnp.arange(capacity, dtype=jnp.int32)
    )
    filled = jnp.any(slot_match, axis=2)
    token_at = jnp.sum(jnp.where(slot_match, tok_iota[None, None, :, None, None], 0), axis=2)
    position = jnp.arange(ctx_size, dtype=jnp.int32)[None, :, None, None] * tok_count + token_at
    position = position.transpose(0, 2, 1, 3).reshape(HEADS, group_count, group_rows)
    filled = filled.transpose(0, 2, 1, 3).reshape(HEADS, group_count, group_rows)

    def group_view(received):
        return received.reshape(HEADS, group_count, group_rows, HEAD_DIM)

    def head_work(operands):
        return attend_groups(
            operands[0], operands[1], operands[2], operands[3], operands[4], operands[5], seq_length
        )

    attended, query_grad, key_grad, value_grad = lax.map(
        head_work,
        (
            group_view(arrived[0]),
            group_view(arrived[1]),
            group_view(arrived[2]),
            group_view(arrived[3]),
            position,
            filled,
        ),
    )

    def owner_view(result):
        return result.reshape(HEADS, 1, C_DEV, ctx_size * capacity, HEAD_DIM)

    returned = (
        lax.all_to_all(owner_view(attended), "ctx", split_axis=3, concat_axis=1, tiled=True),
        lax.all_to_all(owner_view(query_grad), "ctx", split_axis=3, concat_axis=1, tiled=True),
        lax.all_to_all(owner_view(key_grad), "ctx", split_axis=3, concat_axis=1, tiled=True),
        lax.all_to_all(owner_view(value_grad), "ctx", split_axis=3, concat_axis=1, tiled=True),
    )

    def from_slots(slotted):
        flat = slotted.reshape(HEADS, clusters * capacity, HEAD_DIM)
        token_rows = jnp.einsum("hts,hsd->thd", dispatch, flat, preferred_element_type=jnp.float32)
        return token_rows.astype(jnp.bfloat16).reshape(tok_count, HEADS * HEAD_DIM)

    attn_out = from_slots(returned[0])
    q_grad = from_slots(returned[1])
    k_grad = from_slots(returned[2])
    v_grad = from_slots(returned[3])
    layer_out = jnp.dot(attn_out, out_weight, preferred_element_type=jnp.float32).astype(
        jnp.bfloat16
    )
    grad_factor = 1.0 / math.sqrt(tok_count * ctx_size * dp_size)
    shard_sum = lax.psum_scatter(
        lax.dot_general(
            attn_out, cotangent, (((0,), (0,)), ((), ())), preferred_element_type=jnp.float32
        )
        * grad_factor,
        "ctx",
        scatter_dimension=0,
        tiled=True,
    )
    wo_grad = lax.psum(shard_sum, "dp")
    return (layer_out, q_grad, k_grad, v_grad, wo_grad)


def solution(mesh):
    placed = (
        P(("dp", "ctx"), None),
        P(("dp", "ctx"), None),
        P(("dp", "ctx"), None),
        P(("dp", "ctx"), None),
        P(),
        P(None, ("dp", "ctx"), None),
    )
    return jax.shard_map(
        per_device,
        mesh=mesh,
        in_specs=placed,
        out_specs=(
            P(("dp", "ctx"), None),
            P(("dp", "ctx"), None),
            P(("dp", "ctx"), None),
            P(("dp", "ctx"), None),
            P("ctx", None),
        ),
        check_vma=False,
    )
```

profile of v0, /device:TPU:2, one launch (start us, length us, event | category | flops | bytes accessed | tf_op | source)
XLA Modules:
  0.0 985.0 jit_solution(15068401395105552438)
XLA Ops:
  15.1 20.5 %all_to_all.540 = bf16[32,2,8,128]{3,2,1,0:T(8,128)(2,1)} all-to-all(bf16[32,2,8,128]{3,2,1,0:T(8,128)(2,1)S(1)} %bitcast.463), channel_id=1, replica_groups=mesh['dp'=8,'ctx'=32] {'ctx'}, dimensions={0} | all-to-all | bytes 262144 | tf_op jit(solution)/shard_map/all_to_all | solution.py:96
  35.6 14.1 %all_to_all.541 = bf16[32,2,8,128]{3,2,1,0:T(8,128)(2,1)} all-to-all(bf16[32,2,8,128]{3,2,1,0:T(8,128)(2,1)S(1)} %bitcast.461), channel_id=1, replica_groups=mesh['dp'=8,'ctx'=32] {'ctx'}, dimensions={0} | all-to-all | bytes 262144 | tf_op jit(solution)/shard_map/all_to_all | solution.py:96
  49.7 14.3 %all_to_all.542 = bf16[32,2,8,128]{3,2,1,0:T(8,128)(2,1)} all-to-all(bf16[32,2,8,128]{3,2,1,0:T(8,128)(2,1)S(1)} %bitcast.460), channel_id=1, replica_groups=mesh['dp'=8,'ctx'=32] {'ctx'}, dimensions={0} | all-to-all | bytes 262144 | tf_op jit(solution)/shard_map/all_to_all | solution.py:96
  64.0 14.2 %all_to_all.543 = bf16[32,2,8,128]{3,2,1,0:T(8,128)(2,1)} all-to-all(bf16[32,2,8,128]{3,2,1,0:T(8,128)(2,1)S(1)} %bitcast.459), channel_id=1, replica_groups=mesh['dp'=8,'ctx'=32] {'ctx'}, dimensions={0} | all-to-all | bytes 262144 | tf_op jit(solution)/shard_map/all_to_all | solution.py:96
  78.1 14.2 %all_to_all.544 = bf16[32,2,8,128]{3,2,1,0:T(8,128)(2,1)} all-to-all(bf16[32,2,8,128]{3,2,1,0:T(8,128)(2,1)S(1)} %bitcast.458), channel_id=1, replica_groups=mesh['dp'=8,'ctx'=32] {'ctx'}, dimensions={0} | all-to-all | bytes 262144 | tf_op jit(solution)/shard_map/all_to_all | solution.py:96
  92.3 14.2 %all_to_all.545 = bf16[32,2,8,128]{3,2,1,0:T(8,128)(2,1)} all-to-all(bf16[32,2,8,128]{3,2,1,0:T(8,128)(2,1)S(1)} %bitcast.457), channel_id=1, replica_groups=mesh['dp'=8,'ctx'=32] {'ctx'}, dimensions={0} | all-to-all | bytes 262144 | tf_op jit(solution)/shard_map/all_to_all | solution.py:96
  127.4 8.0 all-to-all-done.24
  140.9 43.9 %all_gather.3 = s32[8,8192,1]{1,2,0:T(1,128)S(1)} all-gather(s32[8,256,1]{1,2,0:T(1,128)S(1)} %copy-done.20), channel_id=1, replica_groups=mesh['dp'=8,'ctx'=32] {'ctx'}, dimensions={1}, use_global_device_ids=true | all-gather | bytes 270336 | tf_op jit(solution)/shard_map/all_gather | solution.py:106
  185.5 8.7 all-to-all-start.23
  209.5 9.1 select_reduce_fusion
  218.6 9.9 %all-to-all-start.20 = ((bf16[32,2,8,128]{3,2,1,0:T(8,128)(2,1)}), bf16[32,2,8,128]{3,2,1,0:T(8,128)(2,1)S(1)}, u32[]{:S(2)}, u32[]{:S(2)}) async-start(bf16[32,2,8,128]{3,2,1,0:T(8,128)(2,1)} %bitcast.99), calls=%async_computation.20 | async-start | bytes 262144 | tf_op jit(solution)/shard_map/all_to_all | solution.py:93
  228.7 8.7 all-to-all-done.20
  288.3 8.0 all-to-all-done.16
  296.4 14.8 %all-to-all-start.8 = ((bf16[32,2,8,128]{3,2,1,0:T(8,128)(2,1)}), bf16[32,2,8,128]{3,2,1,0:T(8,128)(2,1)}, u32[]{:S(2)}, u32[]{:S(2)}) async-start(bf16[32,2,8,128]{3,2,1,0:T(8,128)(2,1)} %bitcast.50), calls=%async_computation.8 | async-start | bytes 262144 | tf_op jit(solution)/shard_map/all_to_all | solution.py:90
  311.2 9.1 fusion.71
  322.9 9.9 %all-to-all-start = ((bf16[32,2,8,128]{3,2,1,0:T(8,128)(2,1)}), bf16[32,2,8,128]{3,2,1,0:T(8,128)(2,1)S(1)}, u32[]{:S(2)}, u32[]{:S(2)}) async-start(bf16[32,2,8,128]{3,2,1,0:T(8,128)(2,1)} %bitcast.17), calls=%async_computation | async-start | bytes 262144 | tf_op jit(solution)/shard_map/all_to_all | solution.py:87
  478.9 8.4 all-to-all-done.2
  545.9 85.9 %while.18 = (s32[]{:T(128)}, bf16[8,2,256,128]{3,1,0,2:T(2,128)(2,1)}, bf16[8,2,256,128]{3,1,0,2:T(2,128)(2,1)}, bf16[8,2,256,128]{3,1,0,2:T(2,128)(2,1)}, bf16[...) while((s32[]{:T(128)}, ...), condition=%wide.region_7.8_spmd, body=%wide.region_3.7_spmd.sunk | while | flops 205137152 | bytes 11052245 | solution.py:133
  631.8 28.9 %all_to_all.546 = bf16[8,1,2,256,128]{4,2,0,1,3:T(2,128)(2,1)S(1)} all-to-all(bf16[8,1,2,256,128]{4,2,0,1,3:T(2,128)(2,1)} %bitcast.450), channel_id=1, replica_groups=mesh['dp'=8,'ctx'=32] {'ctx'}, dimensions={3} | all-to-all | bytes 2097152 | tf_op jit(solution)/shard_map/all_to_all | solution.py:149
  668.0 39.7 %all_to_all.547 = bf16[8,1,2,256,128]{4,2,0,1,3:T(2,128)(2,1)} all-to-all(bf16[8,1,2,256,128]{4,2,0,1,3:T(2,128)(2,1)S(1)} %bitcast.447), channel_id=1, replica_groups=mesh['dp'=8,'ctx'=32] {'ctx'}, dimensions={3} | all-to-all | bytes 2097152 | tf_op jit(solution)/shard_map/all_to_all | solution.py:152
  707.7 28.6 %all_to_all.548 = bf16[8,1,2,256,128]{4,2,0,1,3:T(2,128)(2,1)S(1)} all-to-all(bf16[8,1,2,256,128]{4,2,0,1,3:T(2,128)(2,1)S(1)} %bitcast.449), channel_id=1, replica_groups=mesh['dp'=8,'ctx'=32] {'ctx'}, dimensions={3} | all-to-all | bytes 2097152 | tf_op jit(solution)/shard_map/all_to_all | solution.py:150
  746.3 18.9 %all-to-all-done.34 = bf16[8,1,2,256,128]{4,2,0,1,3:T(2,128)(2,1)S(1)} async-done(((bf16[8,1,2,256,128]{4,2,0,1,3:T(2,128)(2,1)}), bf16[8,1,2,256,128]{4,2,0,1,3:T(2,128)(2,1)S(1)}, u32[]{:S(2)}, u32[]{:S(2)}) %all-to-all-start.34) | async-done | bytes 1048608 | tf_op jit(solution)/shard_map/all_to_all | solution.py:151
  771.4 137.6 %reduce-scatter.2.cloned.1.call-done = f32[32,2048]{1,0:T(8,128)} async-done(((f32[1024,2048]{1,0:T(8,128)}), f32[32,2048]{1,0:T(8,128)}) %reduce-scatter.2.cloned.1.call-update) | async-done | bytes 262160 | tf_op jit(solution)/shard_map/reduce_scatter | solution.py:168
  915.2 60.9 %all-reduce.2.cloned.1.call-done = f32[32,2048]{1,0:T(8,128)} async-done(((f32[32,2048]{1,0:T(8,128)}), f32[32,2048]{1,0:T(8,128)}) %all-reduce.2.cloned.1.call-update) | async-done | bytes 262160 | tf_op jit(solution)/shard_map/psum | solution.py:177
  (294 shorter events, 424.8 us)
Async XLA Ops:
  106.6 14.4 %all-to-all-start.25 = ((bf16[32,2,8,128]{3,2,1,0:T(8,128)(2,1)}), bf16[32,2,8,128]{3,2,1,0:T(8,128)(2,1)S(1)}, u32[]{:S(2)}, u32[]{:S(2)}) async-start(bf16[32,2,8,128]{3,2,1,0:T(8,128)(2,1)} %bitcast.120), calls=%async_computation.25 | async-start | bytes 262144 | tf_op jit(solution)/shard_map/all_to_all | solution.py:96
  121.0 14.4 %all-to-all-start.24 = ((bf16[32,2,8,128]{3,2,1,0:T(8,128)(2,1)}), bf16[32,2,8,128]{3,2,1,0:T(8,128)(2,1)S(1)}, u32[]{:S(2)}, u32[]{:S(2)}) async-start(bf16[32,2,8,128]{3,2,1,0:T(8,128)(2,1)} %bitcast.116), calls=%async_computation.24 | async-start | bytes 262144 | tf_op jit(solution)/shard_map/all_to_all | solution.py:96
  135.4 50.1 %all-to-all-start.22 = ((bf16[32,2,8,128]{3,2,1,0:T(8,128)(2,1)}), bf16[32,2,8,128]{3,2,1,0:T(8,128)(2,1)S(1)}, u32[]{:S(2)}, u32[]{:S(2)}) async-start(bf16[32,2,8,128]{3,2,1,0:T(8,128)(2,1)} %bitcast.107), calls=%async_computation.22 | async-start | bytes 262144 | tf_op jit(solution)/shard_map/all_to_all | solution.py:93
  185.5 17.5 %all-to-all-start.23 = ((bf16[32,2,8,128]{3,2,1,0:T(8,128)(2,1)}), bf16[32,2,8,128]{3,2,1,0:T(8,128)(2,1)S(1)}, u32[]{:S(2)}, u32[]{:S(2)}) async-start(bf16[32,2,8,128]{3,2,1,0:T(8,128)(2,1)} %bitcast.111), calls=%async_computation.23 | async-start | bytes 262144 | tf_op jit(solution)/shard_map/all_to_all | solution.py:93
  203.7 14.9 %all-to-all-start.21 = ((bf16[32,2,8,128]{3,2,1,0:T(8,128)(2,1)}), bf16[32,2,8,128]{3,2,1,0:T(8,128)(2,1)S(1)}, u32[]{:S(2)}, u32[]{:S(2)}) async-start(bf16[32,2,8,128]{3,2,1,0:T(8,128)(2,1)} %bitcast.103), calls=%async_computation.21 | async-start | bytes 262144 | tf_op jit(solution)/shard_map/all_to_all | solution.py:93
  218.6 18.8 %all-to-all-start.20 = ((bf16[32,2,8,128]{3,2,1,0:T(8,128)(2,1)}), bf16[32,2,8,128]{3,2,1,0:T(8,128)(2,1)S(1)}, u32[]{:S(2)}, u32[]{:S(2)}) async-start(bf16[32,2,8,128]{3,2,1,0:T(8,128)(2,1)} %bitcast.99), calls=%async_computation.20 | async-start | bytes 262144 | tf_op jit(solution)/shard_map/all_to_all | solution.py:93
  251.7 14.4 %all-to-all-start.18 = ((bf16[32,2,8,128]{3,2,1,0:T(8,128)(2,1)}), bf16[32,2,8,128]{3,2,1,0:T(8,128)(2,1)S(1)}, u32[]{:S(2)}, u32[]{:S(2)}) async-start(bf16[32,2,8,128]{3,2,1,0:T(8,128)(2,1)} %bitcast.91), calls=%async_computation.18 | async-start | bytes 262144 | tf_op jit(solution)/shard_map/all_to_all | solution.py:93
  266.2 15.1 %all-to-all-start.17 = ((bf16[32,2,8,128]{3,2,1,0:T(8,128)(2,1)}), bf16[32,2,8,128]{3,2,1,0:T(8,128)(2,1)}, u32[]{:S(2)}, u32[]{:S(2)}) async-start(bf16[32,2,8,128]{3,2,1,0:T(8,128)(2,1)} %bitcast.87), calls=%async_computation.17 | async-start | bytes 262144 | tf_op jit(solution)/shard_map/all_to_all | solution.py:93
  281.3 15.1 %all-to-all-start.16 = ((bf16[32,2,8,128]{3,2,1,0:T(8,128)(2,1)}), bf16[32,2,8,128]{3,2,1,0:T(8,128)(2,1)}, u32[]{:S(2)}, u32[]{:S(2)}) async-start(bf16[32,2,8,128]{3,2,1,0:T(8,128)(2,1)} %bitcast.83), calls=%async_computation.16 | async-start | bytes 262144 | tf_op jit(solution)/shard_map/all_to_all | solution.py:93
  296.4 26.5 %all-to-all-start.8 = ((bf16[32,2,8,128]{3,2,1,0:T(8,128)(2,1)}), bf16[32,2,8,128]{3,2,1,0:T(8,128)(2,1)}, u32[]{:S(2)}, u32[]{:S(2)}) async-start(bf16[32,2,8,128]{3,2,1,0:T(8,128)(2,1)} %bitcast.50), calls=%async_computation.8 | async-start | bytes 262144 | tf_op jit(solution)/shard_map/all_to_all | solution.py:90
  322.9 18.8 %all-to-all-start = ((bf16[32,2,8,128]{3,2,1,0:T(8,128)(2,1)}), bf16[32,2,8,128]{3,2,1,0:T(8,128)(2,1)S(1)}, u32[]{:S(2)}, u32[]{:S(2)}) async-start(bf16[32,2,8,128]{3,2,1,0:T(8,128)(2,1)} %bitcast.17), calls=%async_computation | async-start | bytes 262144 | tf_op jit(solution)/shard_map/all_to_all | solution.py:87
  341.7 14.5 %all-to-all-start.14 = ((bf16[32,2,8,128]{3,2,1,0:T(8,128)(2,1)}), bf16[32,2,8,128]{3,2,1,0:T(8,128)(2,1)S(1)}, u32[]{:S(2)}, u32[]{:S(2)}) async-start(bf16[32,2,8,128]{3,2,1,0:T(8,128)(2,1)} %bitcast.74), calls=%async_computation.14 | async-start | bytes 262144 | tf_op jit(solution)/shard_map/all_to_all | solution.py:90
  370.6 14.4 %all-to-all-start.13 = ((bf16[32,2,8,128]{3,2,1,0:T(8,128)(2,1)}), bf16[32,2,8,128]{3,2,1,0:T(8,128)(2,1)S(1)}, u32[]{:S(2)}, u32[]{:S(2)}) async-start(bf16[32,2,8,128]{3,2,1,0:T(8,128)(2,1)} %bitcast.70), calls=%async_computation.13 | async-start | bytes 262144 | tf_op jit(solution)/shard_map/all_to_all | solution.py:90
  385.0 14.6 %all-to-all-start.12 = ((bf16[32,2,8,128]{3,2,1,0:T(8,128)(2,1)}), bf16[32,2,8,128]{3,2,1,0:T(8,128)(2,1)S(1)}, u32[]{:S(2)}, u32[]{:S(2)}) async-start(bf16[32,2,8,128]{3,2,1,0:T(8,128)(2,1)} %bitcast.66), calls=%async_computation.12 | async-start | bytes 262144 | tf_op jit(solution)/shard_map/all_to_all | solution.py:90
  428.4 14.5 %all-to-all-start.9 = ((bf16[32,2,8,128]{3,2,1,0:T(8,128)(2,1)}), bf16[32,2,8,128]{3,2,1,0:T(8,128)(2,1)S(1)}, u32[]{:S(2)}, u32[]{:S(2)}) async-start(bf16[32,2,8,128]{3,2,1,0:T(8,128)(2,1)} %bitcast.54), calls=%async_computation.9 | async-start | bytes 262144 | tf_op jit(solution)/shard_map/all_to_all | solution.py:90
  457.3 14.5 %all-to-all-start.4 = ((bf16[32,2,8,128]{3,2,1,0:T(8,128)(2,1)}), bf16[32,2,8,128]{3,2,1,0:T(8,128)(2,1)S(1)}, u32[]{:S(2)}, u32[]{:S(2)}) async-start(bf16[32,2,8,128]{3,2,1,0:T(8,128)(2,1)} %bitcast.33), calls=%async_computation.4 | async-start | bytes 262144 | tf_op jit(solution)/shard_map/all_to_all | solution.py:87
  471.8 15.5 %all-to-all-start.2 = ((bf16[32,2,8,128]{3,2,1,0:T(8,128)(2,1)}), bf16[32,2,8,128]{3,2,1,0:T(8,128)(2,1)S(1)}, u32[]{:S(2)}, u32[]{:S(2)}) async-start(bf16[32,2,8,128]{3,2,1,0:T(8,128)(2,1)} %bitcast.25), calls=%async_computation.2 | async-start | bytes 262144 | tf_op jit(solution)/shard_map/all_to_all | solution.py:87
  487.3 14.7 %all-to-all-start.1 = ((bf16[32,2,8,128]{3,2,1,0:T(8,128)(2,1)}), bf16[32,2,8,128]{3,2,1,0:T(8,128)(2,1)S(1)}, u32[]{:S(2)}, u32[]{:S(2)}) async-start(bf16[32,2,8,128]{3,2,1,0:T(8,128)(2,1)} %bitcast.21), calls=%async_computation.1 | async-start | bytes 262144 | tf_op jit(solution)/shard_map/all_to_all | solution.py:87
  502.0 14.4 %all-to-all-start.3 = ((bf16[32,2,8,128]{3,2,1,0:T(8,128)(2,1)}), bf16[32,2,8,128]{3,2,1,0:T(8,128)(2,1)S(1)}, u32[]{:S(2)}, u32[]{:S(2)}) async-start(bf16[32,2,8,128]{3,2,1,0:T(8,128)(2,1)} %bitcast.29), calls=%async_computation.3 | async-start | bytes 262144 | tf_op jit(solution)/shard_map/all_to_all | solution.py:87
  516.4 14.4 %all-to-all-start.5 = ((bf16[32,2,8,128]{3,2,1,0:T(8,128)(2,1)}), bf16[32,2,8,128]{3,2,1,0:T(8,128)(2,1)S(1)}, u32[]{:S(2)}, u32[]{:S(2)}) async-start(bf16[32,2,8,128]{3,2,1,0:T(8,128)(2,1)} %bitcast.37), calls=%async_computation.5 | async-start | bytes 262144 | tf_op jit(solution)/shard_map/all_to_all | solution.py:87
  530.9 14.4 %all-to-all-start.7 = ((bf16[32,2,8,128]{3,2,1,0:T(8,128)(2,1)}), bf16[32,2,8,128]{3,2,1,0:T(8,128)(2,1)S(1)}, u32[]{:S(2)}, u32[]{:S(2)}) async-start(bf16[32,2,8,128]{3,2,1,0:T(8,128)(2,1)} %bitcast.45), calls=%async_computation.7 | async-start | bytes 262144 | tf_op jit(solution)/shard_map/all_to_all | solution.py:87
  536.3 372.7 %reduce-scatter.2.cloned.1.call-start = ((), (), s32[]{:S(2)}) async-start(), calls=%async_computation.37 | async-start | bytes 8650752 | tf_op jit(solution)/shard_map/reduce_scatter | solution.py:168
  736.3 28.9 %all-to-all-start.34 = ((bf16[8,1,2,256,128]{4,2,0,1,3:T(2,128)(2,1)}), bf16[8,1,2,256,128]{4,2,0,1,3:T(2,128)(2,1)S(1)}, u32[]{:S(2)}, u32[]{:S(2)}) async-start(bf16[8,1,2,256,128]{4,2,0,1,3:T(2,128)(2,1)} %bitcast.448), calls=%async_computation.34 | async-start | bytes 2097152 | tf_op jit(solution)/shard_map/all_to_all | solution.py:151
  741.9 234.2 %all-reduce.2.cloned.1.call-start = ((), (), s32[]{:S(2)}) async-start(), calls=%async_computation.38 | async-start | bytes 524288 | tf_op jit(solution)/shard_map/psum | solution.py:177
  (47 other events, 1802.5 us)
Sparse Core Ops, SparseCore 0:
  668.1 240.8 reduce-scatter.1
  911.3 64.7 all-reduce.1
where the time goes:
time: 997 us; the launch traced here: 985 us
  waiting for transfers between devices  383 us (38%)
  blocking collectives  233 us (23%)
  starting transfers between devices  171 us (17%)
  matrix products  89.7 us (9%)
  local copies, waits for them, and re-layouts  73 us (7%)
  other arithmetic  20 us (2%)
  between operations  15.2 us (2%)
    reduce_scatter x1, waiting for transfers between devices, per_device(): lax.psum_scatter(lax.dot_general(attn_out, cotangent, (((0,), (0,)), ((),...  138 us
    all_to_all x6, blocking collectives, per_device(): lax.all_to_all(grad_slots[head_index], 'ctx', split_axis=0, concat_axis=2...  91.4 us
    psum x1, waiting for transfers between devices, per_device(): wo_grad = lax.psum(shard_sum, 'dp')  60.9 us
    all_to_all x8, waiting for transfers between devices, per_device(): lax.all_to_all(query_slots[head_index], 'ctx', split_axis=0, concat_axis=...  59.1 us
    all_to_all x8, starting transfers between devices, per_device(): lax.all_to_all(key_slots[head_index], 'ctx', split_axis=0, concat_axis=2,...  53.1 us
    all_to_all x8, starting transfers between devices, per_device(): lax.all_to_all(value_slots[head_index], 'ctx', split_axis=0, concat_axis=...  52.8 us
    all_to_all x8, starting transfers between devices, per_device(): lax.all_to_all(query_slots[head_index], 'ctx', split_axis=0, concat_axis=...  48.7 us
    all_to_all x8, waiting for transfers between devices, per_device(): lax.all_to_all(key_slots[head_index], 'ctx', split_axis=0, concat_axis=2,...  47.1 us
  transfers between devices with their start and end apart: 29, of which 26 were waited for; matrix products, arithmetic and copies ran while one was open for 8% of the time, Pallas kernels for 0%

commit v1 on v0

--- a/solution.py
+++ b/solution.py
@@ -174,7 +174,8 @@
         scatter_dimension=0,
         tiled=True,
     )
-    wo_grad = lax.psum(shard_sum, "dp")
+    parts = lax.all_gather(shard_sum, "dp")
+    wo_grad = jnp.sum(parts, axis=0)
     return (layer_out, q_grad, k_grad, v_grad, wo_grad)
 
 

time: 997 us -> 964 us (0.967)
  blocking collectives: 233 us -> 193 us
    reduce_scatter x1, waiting for transfers between devices: 138 us -> 199 us  [per_device(): lax.psum_scatter(lax.dot_general(attn_out, cotangent, (((0,), (0,)), ((),...]
    psum x1 -> x0, waiting for transfers between devices: 60.9 us -> none  [per_device(): wo_grad = lax.psum(shard_sum, 'dp')]
    all_to_all x1 -> x0, blocking collectives: 28.6 us -> none  [per_device(): lax.all_to_all(owner_view(query_grad), 'ctx', split_axis=3, concat_axis=1...]
    unnamed x87 -> x80, local copies, waits for them, and re-layouts: 37.4 us -> 35.3 us
  transfers between devices with their start and end apart: 29 -> 30, of which waited for: 26 -> 25; matrix products, arithmetic and copies ran while one was open for 8% -> 8% of each run, Pallas kernels for 0% -> 0%
where the time goes in v1:
time: 964 us; the launch traced here: 952 us
  waiting for transfers between devices  382 us (40%)
  blocking collectives  193 us (20%)
  starting transfers between devices  179 us (19%)
  matrix products  91.1 us (9%)
  local copies, waits for them, and re-layouts  68.5 us (7%)
  other arithmetic  22.4 us (2%)
  between operations  15.2 us (2%)
    reduce_scatter x1, waiting for transfers between devices, per_device(): lax.psum_scatter(lax.dot_general(attn_out, cotangent, (((0,), (0,)), ((),...  199 us
    all_to_all x6, blocking collectives, per_device(): lax.all_to_all(grad_slots[head_index], 'ctx', split_axis=0, concat_axis=2...  91.4 us
    all_to_all x8, waiting for transfers between devices, per_device(): lax.all_to_all(query_slots[head_index], 'ctx', split_axis=0, concat_axis=...  59 us
    all_to_all x8, starting transfers between devices, per_device(): lax.all_to_all(key_slots[head_index], 'ctx', split_axis=0, concat_axis=2,...  53.1 us
    all_to_all x8, starting transfers between devices, per_device(): lax.all_to_all(value_slots[head_index], 'ctx', split_axis=0, concat_axis=...  52.8 us
    all_to_all x8, starting transfers between devices, per_device(): lax.all_to_all(query_slots[head_index], 'ctx', split_axis=0, concat_axis=...  48.8 us
    all_to_all x8, waiting for transfers between devices, per_device(): lax.all_to_all(key_slots[head_index], 'ctx', split_axis=0, concat_axis=2,...  47 us
    all_gather x1, blocking collectives, per_device(): every_ids = lax.all_gather(cluster_ids, 'ctx', axis=1, tiled=True)  43.9 us
  transfers between devices with their start and end apart: 30, of which 25 were waited for; matrix products, arithmetic and copies ran while one was open for 8% of the time, Pallas kernels for 0%

profile of v1, /device:TPU:2, one launch (start us, length us, event | category | flops | bytes accessed | tf_op | source)
XLA Modules:
  0.0 952.3 jit_solution(3484231713567655390)
XLA Ops:
  15.1 20.5 %all_to_all.540 = bf16[32,2,8,128]{3,2,1,0:T(8,128)(2,1)} all-to-all(bf16[32,2,8,128]{3,2,1,0:T(8,128)(2,1)S(1)} %bitcast.465), channel_id=1, replica_groups=mesh['dp'=8,'ctx'=32] {'ctx'}, dimensions={0} | all-to-all | bytes 262144 | tf_op jit(solution)/shard_map/all_to_all | solution.py:96
  35.6 14.1 %all_to_all.541 = bf16[32,2,8,128]{3,2,1,0:T(8,128)(2,1)} all-to-all(bf16[32,2,8,128]{3,2,1,0:T(8,128)(2,1)S(1)} %bitcast.463), channel_id=1, replica_groups=mesh['dp'=8,'ctx'=32] {'ctx'}, dimensions={0} | all-to-all | bytes 262144 | tf_op jit(solution)/shard_map/all_to_all | solution.py:96
  49.7 14.3 %all_to_all.542 = bf16[32,2,8,128]{3,2,1,0:T(8,128)(2,1)} all-to-all(bf16[32,2,8,128]{3,2,1,0:T(8,128)(2,1)S(1)} %bitcast.462), channel_id=1, replica_groups=mesh['dp'=8,'ctx'=32] {'ctx'}, dimensions={0} | all-to-all | bytes 262144 | tf_op jit(solution)/shard_map/all_to_all | solution.py:96
  64.0 14.2 %all_to_all.543 = bf16[32,2,8,128]{3,2,1,0:T(8,128)(2,1)} all-to-all(bf16[32,2,8,128]{3,2,1,0:T(8,128)(2,1)S(1)} %bitcast.461), channel_id=1, replica_groups=mesh['dp'=8,'ctx'=32] {'ctx'}, dimensions={0} | all-to-all | bytes 262144 | tf_op jit(solution)/shard_map/all_to_all | solution.py:96
  78.1 14.2 %all_to_all.544 = bf16[32,2,8,128]{3,2,1,0:T(8,128)(2,1)} all-to-all(bf16[32,2,8,128]{3,2,1,0:T(8,128)(2,1)S(1)} %bitcast.460), channel_id=1, replica_groups=mesh['dp'=8,'ctx'=32] {'ctx'}, dimensions={0} | all-to-all | bytes 262144 | tf_op jit(solution)/shard_map/all_to_all | solution.py:96
  92.3 14.2 %all_to_all.545 = bf16[32,2,8,128]{3,2,1,0:T(8,128)(2,1)} all-to-all(bf16[32,2,8,128]{3,2,1,0:T(8,128)(2,1)S(1)} %bitcast.459), channel_id=1, replica_groups=mesh['dp'=8,'ctx'=32] {'ctx'}, dimensions={0} | all-to-all | bytes 262144 | tf_op jit(solution)/shard_map/all_to_all | solution.py:96
  127.4 8.0 all-to-all-done.24
  140.9 43.9 %all_gather.9 = s32[8,8192,1]{1,2,0:T(1,128)S(1)} all-gather(s32[8,256,1]{1,2,0:T(1,128)S(1)} %copy-done.18), channel_id=1, replica_groups=mesh['dp'=8,'ctx'=32] {'ctx'}, dimensions={1}, use_global_device_ids=true | all-gather | bytes 270336 | tf_op jit(solution)/shard_map/all_gather | solution.py:106
  185.5 8.7 all-to-all-start.23
  195.3 7.7 all-to-all-done.23
  209.5 9.1 select_reduce_fusion
  218.6 9.9 %all-to-all-start.20 = ((bf16[32,2,8,128]{3,2,1,0:T(8,128)(2,1)}), bf16[32,2,8,128]{3,2,1,0:T(8,128)(2,1)S(1)}, u32[]{:S(2)}, u32[]{:S(2)}) async-start(bf16[32,2,8,128]{3,2,1,0:T(8,128)(2,1)} %bitcast.99), calls=%async_computation.20 | async-start | bytes 262144 | tf_op jit(solution)/shard_map/all_to_all | solution.py:93
  228.7 8.7 all-to-all-done.20
  288.3 8.0 all-to-all-done.16
  296.4 14.8 %all-to-all-start.8 = ((bf16[32,2,8,128]{3,2,1,0:T(8,128)(2,1)}), bf16[32,2,8,128]{3,2,1,0:T(8,128)(2,1)}, u32[]{:S(2)}, u32[]{:S(2)}) async-start(bf16[32,2,8,128]{3,2,1,0:T(8,128)(2,1)} %bitcast.50), calls=%async_computation.8 | async-start | bytes 262144 | tf_op jit(solution)/shard_map/all_to_all | solution.py:90
  311.2 9.1 fusion.71
  322.9 9.9 %all-to-all-start = ((bf16[32,2,8,128]{3,2,1,0:T(8,128)(2,1)}), bf16[32,2,8,128]{3,2,1,0:T(8,128)(2,1)S(1)}, u32[]{:S(2)}, u32[]{:S(2)}) async-start(bf16[32,2,8,128]{3,2,1,0:T(8,128)(2,1)} %bitcast.17), calls=%async_computation | async-start | bytes 262144 | tf_op jit(solution)/shard_map/all_to_all | solution.py:87
  478.9 8.4 all-to-all-done.2
  545.9 85.3 %while.18 = (s32[]{:T(128)}, bf16[8,2,256,128]{3,1,0,2:T(2,128)(2,1)S(1)}, bf16[8,2,256,128]{3,1,0,2:T(2,128)(2,1)}, bf16[8,2,256,128]{3,1,0,2:T(2,128)(2,1)}, b...) while((s32[]{:T(128)}, ...), condition=%wide.region_7.8_spmd, body=%wide.region_3.7_spmd.sunk | while | flops 205137152 | bytes 11052245 | solution.py:133
  631.3 27.5 %all_to_all.546 = bf16[8,1,2,256,128]{4,2,0,1,3:T(2,128)(2,1)S(1)} all-to-all(bf16[8,1,2,256,128]{4,2,0,1,3:T(2,128)(2,1)S(1)} %bitcast.452), channel_id=1, replica_groups=mesh['dp'=8,'ctx'=32] {'ctx'}, dimensions={3} | all-to-all | bytes 2097152 | tf_op jit(solution)/shard_map/all_to_all | solution.py:149
  667.2 30.3 %all_to_all.547 = bf16[8,1,2,256,128]{4,2,0,1,3:T(2,128)(2,1)S(1)} all-to-all(bf16[8,1,2,256,128]{4,2,0,1,3:T(2,128)(2,1)S(1)} %bitcast.449), channel_id=1, replica_groups=mesh['dp'=8,'ctx'=32] {'ctx'}, dimensions={3} | all-to-all | bytes 2097152 | tf_op jit(solution)/shard_map/all_to_all | solution.py:152
  702.6 198.8 %reduce-scatter.2.cloned.1.call-done = f32[32,2048]{1,0:T(8,128)} async-done(((f32[1024,2048]{1,0:T(8,128)}), f32[32,2048]{1,0:T(8,128)}) %reduce-scatter.2.cloned.1.call-update) | async-done | bytes 262160 | tf_op jit(solution)/shard_map/reduce_scatter | solution.py:168
  901.4 8.6 all-to-all-start.34
  915.7 18.4 %all-to-all-done.34 = bf16[8,1,2,256,128]{4,2,0,1,3:T(2,128)(2,1)} async-done(((bf16[8,1,2,256,128]{4,2,0,1,3:T(2,128)(2,1)}), bf16[8,1,2,256,128]{4,2,0,1,3:T(2,128)(2,1)}, u32[]{:S(2)}, u32[]{:S(2)}) %all-to-all-start.34) | async-done | bytes 1048608 | tf_op jit(solution)/shard_map/all_to_all | solution.py:151
  (289 shorter events, 415.4 us)
Async XLA Ops:
  106.5 14.4 %all-to-all-start.25 = ((bf16[32,2,8,128]{3,2,1,0:T(8,128)(2,1)}), bf16[32,2,8,128]{3,2,1,0:T(8,128)(2,1)S(1)}, u32[]{:S(2)}, u32[]{:S(2)}) async-start(bf16[32,2,8,128]{3,2,1,0:T(8,128)(2,1)} %bitcast.120), calls=%async_computation.25 | async-start | bytes 262144 | tf_op jit(solution)/shard_map/all_to_all | solution.py:96
  121.0 14.4 %all-to-all-start.24 = ((bf16[32,2,8,128]{3,2,1,0:T(8,128)(2,1)}), bf16[32,2,8,128]{3,2,1,0:T(8,128)(2,1)S(1)}, u32[]{:S(2)}, u32[]{:S(2)}) async-start(bf16[32,2,8,128]{3,2,1,0:T(8,128)(2,1)} %bitcast.116), calls=%async_computation.24 | async-start | bytes 262144 | tf_op jit(solution)/shard_map/all_to_all | solution.py:96
  135.4 50.1 %all-to-all-start.22 = ((bf16[32,2,8,128]{3,2,1,0:T(8,128)(2,1)}), bf16[32,2,8,128]{3,2,1,0:T(8,128)(2,1)S(1)}, u32[]{:S(2)}, u32[]{:S(2)}) async-start(bf16[32,2,8,128]{3,2,1,0:T(8,128)(2,1)} %bitcast.107), calls=%async_computation.22 | async-start | bytes 262144 | tf_op jit(solution)/shard_map/all_to_all | solution.py:93
  185.5 17.5 %all-to-all-start.23 = ((bf16[32,2,8,128]{3,2,1,0:T(8,128)(2,1)}), bf16[32,2,8,128]{3,2,1,0:T(8,128)(2,1)S(1)}, u32[]{:S(2)}, u32[]{:S(2)}) async-start(bf16[32,2,8,128]{3,2,1,0:T(8,128)(2,1)} %bitcast.111), calls=%async_computation.23 | async-start | bytes 262144 | tf_op jit(solution)/shard_map/all_to_all | solution.py:93
  203.7 14.9 %all-to-all-start.21 = ((bf16[32,2,8,128]{3,2,1,0:T(8,128)(2,1)}), bf16[32,2,8,128]{3,2,1,0:T(8,128)(2,1)S(1)}, u32[]{:S(2)}, u32[]{:S(2)}) async-start(bf16[32,2,8,128]{3,2,1,0:T(8,128)(2,1)} %bitcast.103), calls=%async_computation.21 | async-start | bytes 262144 | tf_op jit(solution)/shard_map/all_to_all | solution.py:93
  218.6 18.8 %all-to-all-start.20 = ((bf16[32,2,8,128]{3,2,1,0:T(8,128)(2,1)}), bf16[32,2,8,128]{3,2,1,0:T(8,128)(2,1)S(1)}, u32[]{:S(2)}, u32[]{:S(2)}) async-start(bf16[32,2,8,128]{3,2,1,0:T(8,128)(2,1)} %bitcast.99), calls=%async_computation.20 | async-start | bytes 262144 | tf_op jit(solution)/shard_map/all_to_all | solution.py:93
  251.7 14.4 %all-to-all-start.18 = ((bf16[32,2,8,128]{3,2,1,0:T(8,128)(2,1)}), bf16[32,2,8,128]{3,2,1,0:T(8,128)(2,1)S(1)}, u32[]{:S(2)}, u32[]{:S(2)}) async-start(bf16[32,2,8,128]{3,2,1,0:T(8,128)(2,1)} %bitcast.91), calls=%async_computation.18 | async-start | bytes 262144 | tf_op jit(solution)/shard_map/all_to_all | solution.py:93
  266.1 15.1 %all-to-all-start.17 = ((bf16[32,2,8,128]{3,2,1,0:T(8,128)(2,1)}), bf16[32,2,8,128]{3,2,1,0:T(8,128)(2,1)}, u32[]{:S(2)}, u32[]{:S(2)}) async-start(bf16[32,2,8,128]{3,2,1,0:T(8,128)(2,1)} %bitcast.87), calls=%async_computation.17 | async-start | bytes 262144 | tf_op jit(solution)/shard_map/all_to_all | solution.py:93
  281.2 15.1 %all-to-all-start.16 = ((bf16[32,2,8,128]{3,2,1,0:T(8,128)(2,1)}), bf16[32,2,8,128]{3,2,1,0:T(8,128)(2,1)}, u32[]{:S(2)}, u32[]{:S(2)}) async-start(bf16[32,2,8,128]{3,2,1,0:T(8,128)(2,1)} %bitcast.83), calls=%async_computation.16 | async-start | bytes 262144 | tf_op jit(solution)/shard_map/all_to_all | solution.py:93
  296.4 26.5 %all-to-all-start.8 = ((bf16[32,2,8,128]{3,2,1,0:T(8,128)(2,1)}), bf16[32,2,8,128]{3,2,1,0:T(8,128)(2,1)}, u32[]{:S(2)}, u32[]{:S(2)}) async-start(bf16[32,2,8,128]{3,2,1,0:T(8,128)(2,1)} %bitcast.50), calls=%async_computation.8 | async-start | bytes 262144 | tf_op jit(solution)/shard_map/all_to_all | solution.py:90
  322.9 18.8 %all-to-all-start = ((bf16[32,2,8,128]{3,2,1,0:T(8,128)(2,1)}), bf16[32,2,8,128]{3,2,1,0:T(8,128)(2,1)S(1)}, u32[]{:S(2)}, u32[]{:S(2)}) async-start(bf16[32,2,8,128]{3,2,1,0:T(8,128)(2,1)} %bitcast.17), calls=%async_computation | async-start | bytes 262144 | tf_op jit(solution)/shard_map/all_to_all | solution.py:87
  341.7 14.5 %all-to-all-start.14 = ((bf16[32,2,8,128]{3,2,1,0:T(8,128)(2,1)}), bf16[32,2,8,128]{3,2,1,0:T(8,128)(2,1)S(1)}, u32[]{:S(2)}, u32[]{:S(2)}) async-start(bf16[32,2,8,128]{3,2,1,0:T(8,128)(2,1)} %bitcast.74), calls=%async_computation.14 | async-start | bytes 262144 | tf_op jit(solution)/shard_map/all_to_all | solution.py:90
  384.9 14.6 %all-to-all-start.12 = ((bf16[32,2,8,128]{3,2,1,0:T(8,128)(2,1)}), bf16[32,2,8,128]{3,2,1,0:T(8,128)(2,1)S(1)}, u32[]{:S(2)}, u32[]{:S(2)}) async-start(bf16[32,2,8,128]{3,2,1,0:T(8,128)(2,1)} %bitcast.66), calls=%async_computation.12 | async-start | bytes 262144 | tf_op jit(solution)/shard_map/all_to_all | solution.py:90
  428.4 14.4 %all-to-all-start.9 = ((bf16[32,2,8,128]{3,2,1,0:T(8,128)(2,1)}), bf16[32,2,8,128]{3,2,1,0:T(8,128)(2,1)S(1)}, u32[]{:S(2)}, u32[]{:S(2)}) async-start(bf16[32,2,8,128]{3,2,1,0:T(8,128)(2,1)} %bitcast.54), calls=%async_computation.9 | async-start | bytes 262144 | tf_op jit(solution)/shard_map/all_to_all | solution.py:90
  457.2 14.5 %all-to-all-start.4 = ((bf16[32,2,8,128]{3,2,1,0:T(8,128)(2,1)}), bf16[32,2,8,128]{3,2,1,0:T(8,128)(2,1)S(1)}, u32[]{:S(2)}, u32[]{:S(2)}) async-start(bf16[32,2,8,128]{3,2,1,0:T(8,128)(2,1)} %bitcast.33), calls=%async_computation.4 | async-start | bytes 262144 | tf_op jit(solution)/shard_map/all_to_all | solution.py:87
  471.7 15.5 %all-to-all-start.2 = ((bf16[32,2,8,128]{3,2,1,0:T(8,128)(2,1)}), bf16[32,2,8,128]{3,2,1,0:T(8,128)(2,1)S(1)}, u32[]{:S(2)}, u32[]{:S(2)}) async-start(bf16[32,2,8,128]{3,2,1,0:T(8,128)(2,1)} %bitcast.25), calls=%async_computation.2 | async-start | bytes 262144 | tf_op jit(solution)/shard_map/all_to_all | solution.py:87
  487.3 14.7 %all-to-all-start.1 = ((bf16[32,2,8,128]{3,2,1,0:T(8,128)(2,1)}), bf16[32,2,8,128]{3,2,1,0:T(8,128)(2,1)S(1)}, u32[]{:S(2)}, u32[]{:S(2)}) async-start(bf16[32,2,8,128]{3,2,1,0:T(8,128)(2,1)} %bitcast.21), calls=%async_computation.1 | async-start | bytes 262144 | tf_op jit(solution)/shard_map/all_to_all | solution.py:87
  502.0 14.4 %all-to-all-start.3 = ((bf16[32,2,8,128]{3,2,1,0:T(8,128)(2,1)}), bf16[32,2,8,128]{3,2,1,0:T(8,128)(2,1)S(1)}, u32[]{:S(2)}, u32[]{:S(2)}) async-start(bf16[32,2,8,128]{3,2,1,0:T(8,128)(2,1)} %bitcast.29), calls=%async_computation.3 | async-start | bytes 262144 | tf_op jit(solution)/shard_map/all_to_all | solution.py:87
  516.4 14.4 %all-to-all-start.5 = ((bf16[32,2,8,128]{3,2,1,0:T(8,128)(2,1)}), bf16[32,2,8,128]{3,2,1,0:T(8,128)(2,1)S(1)}, u32[]{:S(2)}, u32[]{:S(2)}) async-start(bf16[32,2,8,128]{3,2,1,0:T(8,128)(2,1)} %bitcast.37), calls=%async_computation.5 | async-start | bytes 262144 | tf_op jit(solution)/shard_map/all_to_all | solution.py:87
  530.9 14.4 %all-to-all-start.7 = ((bf16[32,2,8,128]{3,2,1,0:T(8,128)(2,1)}), bf16[32,2,8,128]{3,2,1,0:T(8,128)(2,1)S(1)}, u32[]{:S(2)}, u32[]{:S(2)}) async-start(bf16[32,2,8,128]{3,2,1,0:T(8,128)(2,1)} %bitcast.45), calls=%async_computation.7 | async-start | bytes 262144 | tf_op jit(solution)/shard_map/all_to_all | solution.py:87
  536.3 365.1 %reduce-scatter.2.cloned.1.call-start = ((), (), s32[]{:S(2)}) async-start(), calls=%async_computation.37 | async-start | bytes 8650752 | tf_op jit(solution)/shard_map/reduce_scatter | solution.py:168
  697.5 203.9 %all-to-all-start.33 = ((bf16[8,1,2,256,128]{4,2,0,1,3:T(2,128)(2,1)}), bf16[8,1,2,256,128]{4,2,0,1,3:T(2,128)(2,1)S(1)}, u32[]{:S(2)}, u32[]{:S(2)}) async-start(bf16[8,1,2,256,128]{4,2,0,1,3:T(2,128)(2,1)} %bitcast.451), calls=%async_computation.33 | async-start | bytes 2097152 | tf_op jit(solution)/shard_map/all_to_all | solution.py:150
  702.6 240.1 %all-gather.3.cloned.1.call-start = ((), (), s32[]{:S(2)}) async-start(), calls=%async_computation.38 | async-start | bytes 2359296 | tf_op jit(solution)/shard_map/all_gather | solution.py:177
  901.4 32.7 %all-to-all-start.34 = ((bf16[8,1,2,256,128]{4,2,0,1,3:T(2,128)(2,1)}), bf16[8,1,2,256,128]{4,2,0,1,3:T(2,128)(2,1)}, u32[]{:S(2)}, u32[]{:S(2)}) async-start(bf16[8,1,2,256,128]{4,2,0,1,3:T(2,128)(2,1)} %bitcast.450), calls=%async_computation.34 | async-start | bytes 2097152 | tf_op jit(solution)/shard_map/all_to_all | solution.py:151
  (45 other events, 1797.3 us)
Sparse Core Ops, SparseCore 0:
  666.1 235.2 reduce-scatter.1
  903.3 27.0 all-gather.2
